TPU v7x, 128 devices: a whole 4x4x4 slice. The times are simulated.
128 devices in a mesh: row: 8 (over z, y_hi), col: 16 (over x, y_lo, core).
Axes of the slice: x: 4, y: 4 (y_hi: 2, y_lo: 2; y = y_hi * 2 + y_lo), z: 4, core: 2. Of those that a mesh axis runs over, the one named last changes fastest.
Arguments:
- tokens: bfloat16 [1536, 14336], P('col', 'row'), may hold values from -6 to 6
- weight_in: bfloat16 [14336, 14336], P('row', 'col'), may hold values from -0.046875 to 0.046875
- bias_hidden: float32 [14336], P('col'), may hold values from -3 to 3
- weight_out: bfloat16 [14336, 14336], P('col', 'row'), may hold values from -0.046875 to 0.046875
- out_grad: bfloat16 [1536, 14336], P('col', 'row'), may hold values from -0.75 to 0.75
Outputs:
- grad_tokens: bfloat16 [1536, 14336], P('col', 'row')
- grad_weight_in: float32 [14336, 14336], P('row', 'col')
- grad_bias: float32 [14336], P('col')
- grad_weight_out: float32 [14336, 14336], P('col', 'row')
All inputs are finite; a program needn't handle non-finite values.
Results may differ from a plain program's by a relative error of at most 0.007.
Values may be sent and summed in bfloat16 or wider, within the bound.
A program may use at most 128 MiB of HBM per device.

v0:
```python
import jax
import jax.numpy as jnp
from jax import lax
from jax.sharding import PartitionSpec as P

GELU_SCALE = 0.7978845608
GELU_CUBIC = 0.044715


def gelu_parts(values):
    inner = GELU_SCALE * (values + GELU_CUBIC * values * values * values)
    tangent = jnp.tanh(inner)
    result = 0.5 * values * (1.0 + tangent)
    slope = 0.5 * (1.0 + tangent) + 0.5 * values * (1.0 - tangent * tangent) * GELU_SCALE * (
        1.0 + 3.0 * GELU_CUBIC * values * values
    )
    return (result, slope)


def contract_rows(left, right):
    return lax.dot_general(
        left, right, (((0,), (0,)), ((), ())), preferred_element_type=jnp.float32
    )


def contract_cols(left, right):
    return lax.dot_general(
        left, right, (((1,), (1,)), ((), ())), preferred_element_type=jnp.float32
    )


def local(tokens, weight_in, bias_hidden, weight_out, out_grad):
    tok_all, grad_all = (
        lax.all_gather(tokens, "col", axis=0, tiled=True),
        lax.all_gather(out_grad, "col", axis=0, tiled=True),
    )
    pre_part = jnp.dot(tok_all, weight_in, preferred_element_type=jnp.float32)
    act_part = contract_cols(grad_all, weight_out)
    pre_mine, act_mine = (
        lax.psum_scatter(pre_part, "row", scatter_dimension=0, tiled=True),
        lax.psum_scatter(act_part, "row", scatter_dimension=0, tiled=True),
    )
    result, slope = gelu_parts(pre_mine + bias_hidden)
    act_local = result.astype(jnp.bfloat16)
    pre_grad_local = (act_mine * slope).astype(jnp.bfloat16)
    bias_local = jnp.sum(pre_grad_local, axis=0, dtype=jnp.float32)
    act_all, pre_grad_all = (
        lax.all_gather(act_local, "row", axis=0, tiled=True),
        lax.all_gather(pre_grad_local, "row", axis=0, tiled=True),
    )
    grad_bias = lax.psum(bias_local, "row")
    grad_weight_out = contract_rows(act_all, grad_all)
    grad_weight_in = contract_rows(tok_all, pre_grad_all)
    grad_tokens = lax.psum_scatter(
        contract_cols(pre_grad_all, weight_in), "col", scatter_dimension=0, tiled=True
    ).astype(jnp.bfloat16)
    return (grad_tokens, grad_weight_in, grad_bias, grad_weight_out)


def solution(mesh):
    placed = (P("col", "row"), P("row", "col"), P("col"), P("col", "row"), P("col", "row"))
    return jax.shard_map(
        local,
        mesh=mesh,
        in_specs=placed,
        out_specs=(P("col", "row"), P("row", "col"), P("col"), P("col", "row")),
        check_vma=False,
    )
```

profile of v0, /device:TPU:1, one launch (start us, length us, event | category | flops | bytes accessed | tf_op | source)
XLA Modules:
  0.0 540.9 jit_solution(17161725866408645790)
XLA Ops:
  7.2 0.0 copy-start
  7.2 0.0 all-gather.5.cloned.1.call-start
  7.2 0.7 all-gather.5.cloned.1.call-update
  7.9 0.0 all-gather.7.cloned.1.call-start
  8.0 0.7 all-gather.7.cloned.1.call-update
  8.7 0.0 reduce-scatter.4.cloned.1.call-start
  8.7 44.7 %all-gather.5.cloned.1.call-done = bf16[1536,1792]{1,0:T(8,128)(2,1)} async-done(((bf16[96,1792]{1,0:T(8,128)(2,1)}), bf16[1536,1792]{1,0:T(8,128)(2,1)}) %all-gather.5.cloned.1.call-update) | async-done | bytes 5505040 | tf_op jit(solution)/shard_map/all_gather | solution.py:35
  53.4 10.3 %fusion.8 = f32[1536,896]{1,0:T(8,128)} fusion(bf16[1536,1792]{1,0:T(8,128)(2,1)} %all-gather.5.cloned.1.call-done, bf16[896,1792]{1,0:T(8,128)(2,1)} %param.8), kind=kOutput, calls=%fused_computation.12 | convolution fusion | flops 4932501504 | bytes 14221312 | tf_op jit(solution)/shard_map/dot_general | solution.py:27
  63.8 0.0 reduce-scatter.4.cloned.1.call-update
  63.8 0.0 reduce-scatter.6.cloned.1.call-start
  63.8 31.1 %all-gather.7.cloned.1.call-done = bf16[1536,1792]{1,0:T(8,128)(2,1)} async-done(((bf16[96,1792]{1,0:T(8,128)(2,1)}), bf16[1536,1792]{1,0:T(8,128)(2,1)}) %all-gather.7.cloned.1.call-update) | async-done | bytes 5505040 | tf_op jit(solution)/shard_map/all_gather | solution.py:34
  94.9 0.0 copy-done
  94.9 9.3 %fusion.9 = f32[1536,896]{1,0:T(8,128)} fusion(bf16[1536,1792]{1,0:T(8,128)(2,1)} %all-gather.7.cloned.1.call-done, bf16[1792,896]{1,0:T(8,128)(2,1)S(1)} %copy-done), kind=kOutput, calls=%fused_computation.13 | convolution fusion | flops 4932501504 | bytes 14221312 | tf_op jit(solution)/shard_map/dot_general | solution.py:37
  104.2 0.0 copy-start.2
  104.3 0.0 reduce-scatter.6.cloned.1.call-update
  104.3 0.0 all-gather.9.cloned.1.call-start
  104.3 86.9 %reduce-scatter.4.cloned.1.call-done = f32[192,896]{1,0:T(8,128)} async-done(((f32[1536,896]{1,0:T(8,128)}), f32[192,896]{1,0:T(8,128)}) %reduce-scatter.4.cloned.1.call-update) | async-done | bytes 688144 | tf_op jit(solution)/shard_map/reduce_scatter | solution.py:41
  191.2 96.3 %reduce-scatter.6.cloned.1.call-done = f32[192,896]{1,0:T(8,128)} async-done(((f32[1536,896]{1,0:T(8,128)}), f32[192,896]{1,0:T(8,128)}) %reduce-scatter.6.cloned.1.call-update) | async-done | bytes 688144 | tf_op jit(solution)/shard_map/reduce_scatter | solution.py:40
  287.5 0.0 copy-done.2
  287.5 2.7 convert_reduce_fusion
  290.2 0.0 all-gather.9.cloned.1.call-update
  290.2 0.0 all-gather.11.cloned.1.call-start
  290.3 0.5 all-gather.11.cloned.1.call-update
  290.8 0.0 reduce-scatter.8.cloned.1.call-start
  290.8 57.9 %all-gather.9.cloned.1.call-done = bf16[1536,896]{1,0:T(8,128)(2,1)} async-done(((bf16[192,896]{1,0:T(8,128)(2,1)}), bf16[1536,896]{1,0:T(8,128)(2,1)}) %all-gather.9.cloned.1.call-update) | async-done | bytes 2752528 | tf_op jit(solution)/shard_map/all_gather | solution.py:49
  348.8 9.9 %fusion.10 = f32[1536,1792]{1,0:T(8,128)} fusion(bf16[1536,896]{1,0:T(8,128)(2,1)} %all-gather.9.cloned.1.call-done, bf16[1792,896]{1,0:T(8,128)(2,1)S(1)} %copy-done), kind=kOutput, calls=%fused_computation.14 | convolution fusion | flops 4932501504 | bytes 16973824 | tf_op jit(solution)/shard_map/dot_general | solution.py:27
  358.7 0.0 copy-start.3
  358.7 0.0 reduce-scatter.8.cloned.1.call-update
  358.7 17.6 %psum.7 = f32[896]{0:T(1024)} all-reduce(f32[896]{0:T(1024)S(1)} %get-tuple-element.8), channel_id=1, replica_groups=mesh['row'=8,'col'=16] {'row'}, use_global_device_ids=true, to_apply=%region_4.0 | all-reduce | flops 896 | bytes 7168 | tf_op jit(solution)/shard_map/psum | solution.py:51
  376.3 0.0 copy-done.3
  376.3 10.5 %convolution_bitcast_fusion = f32[1792,896]{0,1:T(8,128)} fusion(bf16[1536,896]{1,0:T(8,128)(2,1)S(1)} %copy-done.3, bf16[1536,1792]{1,0:T(8,128)(2,1)} %all-gather.7.cloned.1.call-done), kind=kOutput, calls=%fused_computation | convolution fusion | flops 4932501504 | bytes 14680064 | tf_op jit(solution)/shard_map/dot_general | solution.py:21
  386.8 0.0 copy-start.1
  386.8 8.0 %copy.9 = f32[1792,896]{1,0:T(8,128)} copy(f32[1792,896]{0,1:T(8,128)} %convolution_bitcast_fusion) | data formatting | bytes 12845056
  394.8 13.5 %all-gather.11.cloned.1.call-done = bf16[1536,896]{1,0:T(8,128)(2,1)} async-done(((bf16[192,896]{1,0:T(8,128)(2,1)}), bf16[1536,896]{1,0:T(8,128)(2,1)}) %all-gather.11.cloned.1.call-update) | async-done | bytes 2752528 | tf_op jit(solution)/shard_map/all_gather | solution.py:48
  408.3 11.4 %fusion.11 = f32[896,1792]{1,0:T(8,128)} fusion(bf16[1536,896]{1,0:T(8,128)(2,1)} %all-gather.11.cloned.1.call-done, bf16[1536,1792]{1,0:T(8,128)(2,1)} %all-gather.5.cloned.1.call-done), kind=kOutput, calls=%fused_computation.15 | convolution fusion | flops 4932501504 | bytes 14680064 | tf_op jit(solution)/shard_map/dot_general | solution.py:21
  419.7 112.5 %reduce-scatter.8.cloned.1.call-done = f32[96,1792]{1,0:T(8,128)} async-done(((f32[1536,1792]{1,0:T(8,128)}), f32[96,1792]{1,0:T(8,128)}) %reduce-scatter.8.cloned.1.call-update) | async-done | bytes 688144 | tf_op jit(solution)/shard_map/reduce_scatter | solution.py:54
  532.2 1.9 convert_element_type.13
  534.0 0.0 copy-done.1
Async XLA Ops:
  7.2 87.8 %copy-start = (bf16[1792,896]{1,0:T(8,128)(2,1)S(1)}, bf16[1792,896]{1,0:T(8,128)(2,1)}, u32[]{:S(2)}) copy-start(bf16[1792,896]{1,0:T(8,128)(2,1)} %param.6) | copy-start | bytes 9633796
  7.2 46.2 %all-gather.5.cloned.1.call-start = ((), (), s32[]{:S(2)}) async-start(), calls=%async_computation.3 | async-start | bytes 5849088 | tf_op jit(solution)/shard_map/all_gather | solution.py:35
  7.9 87.0 %all-gather.7.cloned.1.call-start = ((), (), s32[]{:S(2)}) async-start(), calls=%async_computation.5 | async-start | bytes 5849088 | tf_op jit(solution)/shard_map/all_gather | solution.py:34
  8.7 182.5 %reduce-scatter.4.cloned.1.call-start = ((), (), s32[]{:S(2)}) async-start(), calls=%async_computation.4 | async-start | bytes 6193152 | tf_op jit(solution)/shard_map/reduce_scatter | solution.py:41
  63.8 223.7 %reduce-scatter.6.cloned.1.call-start = ((), (), s32[]{:S(2)}) async-start(), calls=%async_computation.6 | async-start | bytes 6193152 | tf_op jit(solution)/shard_map/reduce_scatter | solution.py:40
  104.2 183.3 %copy-start.2 = (f32[896]{0:T(1024)S(1)}, f32[896]{0:T(1024)}, u32[]{:S(2)}) copy-start(f32[896]{0:T(1024)} %param.7) | copy-start | bytes 10756
  104.3 244.5 %all-gather.9.cloned.1.call-start = ((), (), s32[]{:S(2)}) async-start(), calls=%async_computation.7 | async-start | bytes 3096576 | tf_op jit(solution)/shard_map/all_gather | solution.py:49
  290.2 118.1 %all-gather.11.cloned.1.call-start = ((), (), s32[]{:S(2)}) async-start(), calls=%async_computation.9 | async-start | bytes 3096576 | tf_op jit(solution)/shard_map/all_gather | solution.py:48
  290.8 241.4 %reduce-scatter.8.cloned.1.call-start = ((), (), s32[]{:S(2)}) async-start(), calls=%async_computation.8 | async-start | bytes 11698176 | tf_op jit(solution)/shard_map/reduce_scatter | solution.py:54
  358.7 17.6 %copy-start.3 = (bf16[1536,896]{1,0:T(8,128)(2,1)S(1)}, bf16[1536,896]{1,0:T(8,128)(2,1)}, u32[]{:S(2)}) copy-start(bf16[1536,896]{1,0:T(8,128)(2,1)} %all-gather.9.cloned.1.call-done) | copy-start | bytes 8257540
  386.8 147.2 %copy-start.1 = (bf16[1792,896]{1,0:T(8,128)(2,1)S(1)}, bf16[1792,896]{1,0:T(8,128)(2,1)}, u32[]{:S(2)}) copy-start(bf16[1792,896]{1,0:T(8,128)(2,1)} %param.6) | copy-start | bytes 9633796
Sparse Core Ops, SparseCore 0:
  9.7 43.6 all-gather.4
  55.1 39.7 all-gather.6
  99.4 91.7 reduce-scatter.3
  196.0 91.4 reduce-scatter.5
  290.3 58.3 all-gather.8
  350.9 57.3 all-gather.10
  410.7 121.3 reduce-scatter.7
where the time goes:
time: 541 us
  waiting for transfers between devices  445 us (82%)
  matrix products  51.5 us (10%)
  blocking collectives  17.6 us (3%)
  between operations  14.1 us (3%)
  local copies, waits for them, and re-layouts  7.99 us (1%)
    reduce_scatter x1, waiting for transfers between devices, local(): lax.psum_scatter(contract_cols(pre_grad_all, weight_in), 'col', scatter_d...  112 us
    reduce_scatter x1, waiting for transfers between devices, local(): lax.psum_scatter(pre_part, 'row', scatter_dimension=0, tiled=True)  96.3 us
    reduce_scatter x1, waiting for transfers between devices, local(): lax.psum_scatter(act_part, 'row', scatter_dimension=0, tiled=True)  86.9 us
    all_gather x1, waiting for transfers between devices, local(): lax.all_gather(pre_grad_local, 'row', axis=0, tiled=True)  57.9 us
    all_gather x1, waiting for transfers between devices, local(): lax.all_gather(out_grad, 'col', axis=0, tiled=True)  44.7 us
    all_gather x1, waiting for transfers between devices, local(): lax.all_gather(tokens, 'col', axis=0, tiled=True)  31.1 us
    dot_general x2, matrix products, contract_rows(): lax.dot_general(left, right, (((0,), (0,)), ((), ())), preferred_element_...  21.9 us
    dot_general x2, matrix products, contract_cols(): lax.dot_general(left, right, (((1,), (1,)), ((), ())), preferred_element_...  20.2 us
  transfers between devices with their start and end apart: 7, of which 7 were waited for; matrix products, arithmetic and copies ran while one was open for 11% of the time, Pallas kernels for 0%

commit v1 on v0

--- a/solution.py
+++ b/solution.py
@@ -31,7 +31,9 @@
 
 def local(tokens, weight_in, bias_hidden, weight_out, out_grad):
     tok_all, grad_all = (
-        lax.all_gather(tokens, "col", axis=0, tiled=True),
+        jnp.concatenate(
+            lax.all_to_all(jnp.stack([tokens] * lax.axis_size("col")), "col", 0, 0), axis=0
+        ),
         lax.all_gather(out_grad, "col", axis=0, tiled=True),
     )
     pre_part = jnp.dot(tok_all, weight_in, preferred_element_type=jnp.float32)

time: 541 us -> 520 us (0.961)
  waiting for transfers between devices: 445 us -> 317 us
  blocking collectives: 17.6 us -> 119 us
    all_to_all x0 -> x1, blocking collectives: none -> 95.1 us  [local(): lax.all_to_all(jnp.stack([tokens] * lax.axis_size('col')), 'col', 0, 0)]
    all_gather x1, waiting for transfers between devices: 44.7 us -> 0.02 us  [local(): lax.all_gather(out_grad, 'col', axis=0, tiled=True)]
    reduce_scatter x1, waiting for transfers between devices: 112 us -> 68.5 us  [local(): lax.psum_scatter(contract_cols(pre_grad_all, weight_in), 'col', scatter_d...]
    all_gather x1 -> x0, waiting for transfers between devices: 31.1 us -> none  [local(): lax.all_gather(tokens, 'col', axis=0, tiled=True)]
    reduce_scatter x1, waiting for transfers between devices: 96.3 us -> 81.3 us  [local(): lax.psum_scatter(pre_part, 'row', scatter_dimension=0, tiled=True)]
    reduce_scatter x1, waiting for transfers between devices: 86.9 us -> 95.8 us  [local(): lax.psum_scatter(act_part, 'row', scatter_dimension=0, tiled=True)]
    psum x1, blocking collectives: 17.6 us -> 23.8 us  [local(): grad_bias = lax.psum(bias_local, 'row')]
  transfers between devices with their start and end apart: 7 -> 6, of which waited for: 7 -> 5; matrix products, arithmetic and copies ran while one was open for 11% -> 12% of each run, Pallas kernels for 0% -> 0%
where the time goes in v1:
time: 520 us
  waiting for transfers between devices  317 us (61%)
  blocking collectives  119 us (23%)
  matrix products  50.9 us (10%)
  between operations  15.7 us (3%)
  local copies, waits for them, and re-layouts  11.9 us (2%)
    reduce_scatter x1, waiting for transfers between devices, local(): lax.psum_scatter(act_part, 'row', scatter_dimension=0, tiled=True)  95.8 us
    all_to_all x1, blocking collectives, local(): lax.all_to_all(jnp.stack([tokens] * lax.axis_size('col')), 'col', 0, 0)  95.1 us
    reduce_scatter x1, waiting for transfers between devices, local(): lax.psum_scatter(pre_part, 'row', scatter_dimension=0, tiled=True)  81.3 us
    reduce_scatter x1, waiting for transfers between devices, local(): lax.psum_scatter(contract_cols(pre_grad_all, weight_in), 'col', scatter_d...  68.5 us
    all_gather x1, waiting for transfers between devices, local(): lax.all_gather(pre_grad_local, 'row', axis=0, tiled=True)  57.4 us
    psum x1, blocking collectives, local(): grad_bias = lax.psum(bias_local, 'row')  23.8 us
    dot_general x2, matrix products, contract_rows(): lax.dot_general(left, right, (((0,), (0,)), ((), ())), preferred_element_...  23.1 us
    dot_general x2, matrix products, contract_cols(): lax.dot_general(left, right, (((1,), (1,)), ((), ())), preferred_element_...  20.3 us
  transfers between devices with their start and end apart: 6, of which 5 were waited for; matrix products, arithmetic and copies ran while one was open for 12% of the time, Pallas kernels for 0%

profile of v1, /device:TPU:1, one launch (start us, length us, event | category | flops | bytes accessed | tf_op | source)
XLA Modules:
  0.0 519.6 jit_solution(8241186705899221400)
XLA Ops:
  8.0 0.0 copy-start
  8.0 0.0 all-gather.4.cloned.1.call-start
  8.1 0.7 all-gather.4.cloned.1.call-update
  8.7 0.0 reduce-scatter.6.cloned.1.call-start
  8.8 1.7 stack.2
  10.5 95.1 %all_to_all.5 = bf16[16,96,1792]{2,1,0:T(8,128)(2,1)S(1)} all-to-all(bf16[16,96,1792]{2,1,0:T(8,128)(2,1)S(1)} %stack.2), channel_id=1, replica_groups=mesh['row'=8,'col'=16] {'col'}, dimensions={0} | all-to-all | bytes 11010048 | tf_op jit(solution)/shard_map/all_to_all | solution.py:35
  105.5 0.0 copy-start.1
  105.5 2.4 copy-done.1
  107.9 0.0 copy-done
  107.9 7.6 %fusion.9 = f32[1536,896]{1,0:T(8,128)} fusion(bf16[1536,1792]{1,0:T(8,128)(2,1)S(1)} %bitcast.13, bf16[1792,896]{1,0:T(8,128)(2,1)S(1)} %copy-done), kind=kOutput, calls=%fused_computation.13 | convolution fusion | flops 4932501504 | bytes 14221312 | tf_op jit(solution)/shard_map/dot_general | solution.py:39
  115.5 0.0 reduce-scatter.6.cloned.1.call-update
  115.5 0.0 reduce-scatter.4.cloned.1.call-start
  115.6 0.0 all-gather.4.cloned.1.call-done
  115.6 10.4 %fusion.8 = f32[1536,896]{1,0:T(8,128)} fusion(bf16[1536,1792]{1,0:T(8,128)(2,1)} %all-gather.4.cloned.1.call-done, bf16[896,1792]{1,0:T(8,128)(2,1)} %param.8), kind=kOutput, calls=%fused_computation.12 | convolution fusion | flops 4932501504 | bytes 14221312 | tf_op jit(solution)/shard_map/dot_general | solution.py:27
  126.0 0.0 copy-start.2
  126.0 0.0 reduce-scatter.4.cloned.1.call-update
  126.0 0.0 all-gather.6.cloned.1.call-start
  126.0 81.3 %reduce-scatter.6.cloned.1.call-done = f32[192,896]{1,0:T(8,128)} async-done(((f32[1536,896]{1,0:T(8,128)}), f32[192,896]{1,0:T(8,128)}) %reduce-scatter.6.cloned.1.call-update) | async-done | bytes 688144 | tf_op jit(solution)/shard_map/reduce_scatter | solution.py:42
  207.3 95.8 %reduce-scatter.4.cloned.1.call-done = f32[192,896]{1,0:T(8,128)} async-done(((f32[1536,896]{1,0:T(8,128)}), f32[192,896]{1,0:T(8,128)}) %reduce-scatter.4.cloned.1.call-update) | async-done | bytes 688144 | tf_op jit(solution)/shard_map/reduce_scatter | solution.py:43
  303.1 0.0 copy-done.2
  303.1 2.7 convert_reduce_fusion
  305.8 0.0 all-gather.6.cloned.1.call-update
  305.8 0.0 all-gather.8.cloned.1.call-start
  305.8 0.7 all-gather.8.cloned.1.call-update
  306.5 0.0 reduce-scatter.8.cloned.1.call-start
  306.6 57.4 %all-gather.6.cloned.1.call-done = bf16[1536,896]{1,0:T(8,128)(2,1)} async-done(((bf16[192,896]{1,0:T(8,128)(2,1)}), bf16[1536,896]{1,0:T(8,128)(2,1)}) %all-gather.6.cloned.1.call-update) | async-done | bytes 2752528 | tf_op jit(solution)/shard_map/all_gather | solution.py:51
  363.9 9.9 %fusion.10 = f32[1536,1792]{1,0:T(8,128)} fusion(bf16[1536,896]{1,0:T(8,128)(2,1)} %all-gather.6.cloned.1.call-done, bf16[1792,896]{1,0:T(8,128)(2,1)S(1)} %copy-done), kind=kOutput, calls=%fused_computation.14 | convolution fusion | flops 4932501504 | bytes 16973824 | tf_op jit(solution)/shard_map/dot_general | solution.py:27
  373.8 0.0 reduce-scatter.8.cloned.1.call-update
  373.9 23.8 %psum.7 = f32[896]{0:T(1024)} all-reduce(f32[896]{0:T(1024)S(1)} %get-tuple-element.8), channel_id=1, replica_groups=mesh['row'=8,'col'=16] {'row'}, use_global_device_ids=true, to_apply=%region_4.0 | all-reduce | flops 896 | bytes 7168 | tf_op jit(solution)/shard_map/psum | solution.py:53
  397.6 11.6 %convolution_bitcast_fusion = f32[1792,896]{0,1:T(8,128)} fusion(bf16[1536,896]{1,0:T(8,128)(2,1)} %all-gather.6.cloned.1.call-done, bf16[1536,1792]{1,0:T(8,128)(2,1)} %bitcast.14), kind=kOutput, calls=%fused_computation | convolution fusion | flops 4932501504 | bytes 14680064 | tf_op jit(solution)/shard_map/dot_general | solution.py:21
  409.2 7.8 %copy.9 = f32[1792,896]{1,0:T(8,128)} copy(f32[1792,896]{0,1:T(8,128)} %convolution_bitcast_fusion) | data formatting | bytes 12845056
  417.0 13.2 %all-gather.8.cloned.1.call-done = bf16[1536,896]{1,0:T(8,128)(2,1)} async-done(((bf16[192,896]{1,0:T(8,128)(2,1)}), bf16[1536,896]{1,0:T(8,128)(2,1)}) %all-gather.8.cloned.1.call-update) | async-done | bytes 2752528 | tf_op jit(solution)/shard_map/all_gather | solution.py:50
  430.2 11.5 %fusion.11 = f32[896,1792]{1,0:T(8,128)} fusion(bf16[1536,896]{1,0:T(8,128)(2,1)} %all-gather.8.cloned.1.call-done, bf16[1536,1792]{1,0:T(8,128)(2,1)} %all-gather.4.cloned.1.call-done), kind=kOutput, calls=%fused_computation.15 | convolution fusion | flops 4932501504 | bytes 14680064 | tf_op jit(solution)/shard_map/dot_general | solution.py:21
  441.6 68.5 %reduce-scatter.8.cloned.1.call-done = f32[96,1792]{1,0:T(8,128)} async-done(((f32[1536,1792]{1,0:T(8,128)}), f32[96,1792]{1,0:T(8,128)}) %reduce-scatter.8.cloned.1.call-update) | async-done | bytes 688144 | tf_op jit(solution)/shard_map/reduce_scatter | solution.py:56
  510.1 1.9 convert_element_type.13
Async XLA Ops:
  8.0 99.9 %copy-start = (bf16[1792,896]{1,0:T(8,128)(2,1)S(1)}, bf16[1792,896]{1,0:T(8,128)(2,1)}, u32[]{:S(2)}) copy-start(bf16[1792,896]{1,0:T(8,128)(2,1)} %param.6) | copy-start | bytes 9633796
  8.0 107.6 %all-gather.4.cloned.1.call-start = ((), (), s32[]{:S(2)}) async-start(), calls=%async_computation.4 | async-start | bytes 5849088 | tf_op jit(solution)/shard_map/all_gather | solution.py:37
  8.7 198.6 %reduce-scatter.6.cloned.1.call-start = ((), (), s32[]{:S(2)}) async-start(), calls=%async_computation.6 | async-start | bytes 6193152 | tf_op jit(solution)/shard_map/reduce_scatter | solution.py:42
  105.5 2.4 copy-start.1
  115.5 187.6 %reduce-scatter.4.cloned.1.call-start = ((), (), s32[]{:S(2)}) async-start(), calls=%async_computation.5 | async-start | bytes 6193152 | tf_op jit(solution)/shard_map/reduce_scatter | solution.py:43
  126.0 177.1 %copy-start.2 = (f32[896]{0:T(1024)S(1)}, f32[896]{0:T(1024)}, u32[]{:S(2)}) copy-start(f32[896]{0:T(1024)} %param.7) | copy-start | bytes 10756
  126.0 237.9 %all-gather.6.cloned.1.call-start = ((), (), s32[]{:S(2)}) async-start(), calls=%async_computation.7 | async-start | bytes 3096576 | tf_op jit(solution)/shard_map/all_gather | solution.py:51
  305.8 124.4 %all-gather.8.cloned.1.call-start = ((), (), s32[]{:S(2)}) async-start(), calls=%async_computation.9 | async-start | bytes 3096576 | tf_op jit(solution)/shard_map/all_gather | solution.py:50
  306.5 203.6 %reduce-scatter.8.cloned.1.call-start = ((), (), s32[]{:S(2)}) async-start(), calls=%async_computation.8 | async-start | bytes 11698176 | tf_op jit(solution)/shard_map/reduce_scatter | solution.py:56
Sparse Core Ops, SparseCore 0:
  10.6 95.8 all-gather.3
  374.0 136.0 reduce-scatter.7
Sparse Core Ops, SparseCore 1:
  115.6 91.7 reduce-scatter.5
  212.1 90.9 reduce-scatter.3
  305.9 58.0 all-gather.5
  366.2 63.9 all-gather.7
